TPU v7x, 128 devices: a whole 4x4x4 slice. The times are simulated.
128 devices in a mesh: dp: 16 (over x_lo, y, core), tensor: 8 (over x_hi, z).
Axes of the slice: x: 4 (x_hi: 2, x_lo: 2; x = x_hi * 2 + x_lo), y: 4, z: 4, core: 2. Of those that a mesh axis runs over, the one named last changes fastest.
Arguments:
- block_input: bfloat16 [32768, 768], P(('dp', 'tensor')), may hold values from -6 to 6
- w_value: bfloat16 [768, 768], replicated, may hold values from -0.21875 to 0.21875
- b_value: bfloat16 [768], replicated, may hold values from -2 to 2
- conv_kernel: bfloat16 [65, 768], replicated, may hold values from -0.75 to 0.75
- w_out: bfloat16 [768, 768], replicated, may hold values from -0.21875 to 0.21875
- b_out: bfloat16 [768], replicated, may hold values from -2 to 2
- gain_attn: bfloat16 [768], replicated, may hold values from 0.5 to 1.5
- shift_attn: bfloat16 [768], replicated, may hold values from -2 to 2
- w_up: bfloat16 [768, 3072], P(None, 'tensor'), may hold values from -0.21875 to 0.21875
- b_up: bfloat16 [3072], P('tensor'), may hold values from -2 to 2
- w_down: bfloat16 [3072, 768], P('tensor'), may hold values from -0.109375 to 0.109375
- b_down: bfloat16 [768], replicated, may hold values from -2 to 2
- gain_ffn: bfloat16 [768], replicated, may hold values from 0.5 to 1.5
- shift_ffn: bfloat16 [768], replicated, may hold values from -2 to 2
- query_codes: int32 [32768, 384], P(('dp', 'tensor')), may hold values from 0 to 255
- key_codes: int32 [32768, 384], P(('dp', 'tensor')), may hold values from 0 to 255
- key_live: int32 [32768], P(('dp', 'tensor')), may hold values 0 or 1
- seq_lengths: int32 [128, 4], P(('dp', 'tensor')), may hold values from 1 to 128, 256 in all within a row
- out_grad: bfloat16 [32768, 768], P(('dp', 'tensor')), may hold values from -6 to 6
Outputs:
- block_output: bfloat16 [32768, 768], P(('dp', 'tensor'))
- input_grad: float32 [32768, 768], P(('dp', 'tensor'))
- grad_w_value: float32 [768, 768], replicated
- grad_b_value: float32 [768], replicated
- grad_conv_kernel: float32 [65, 768], replicated
- grad_w_out: float32 [768, 768], replicated
- grad_b_out: float32 [768], replicated
- grad_gain_attn: float32 [768], replicated
- grad_shift_attn: float32 [768], replicated
- grad_w_up: float32 [768, 3072], P(None, 'tensor')
- grad_b_up: float32 [3072], P('tensor')
- grad_w_down: float32 [3072, 768], P('tensor')
- grad_b_down: float32 [768], replicated
- grad_gain_ffn: float32 [768], replicated
- grad_shift_ffn: float32 [768], replicated
Inputs may be any that keep to these rules, and one draw needn't show every extreme that they name: `seq_lengths`: each item's lengths sum to 256; the longest is 128. `key_live`: 1 marks a live key, 0 a padded one. `query_codes`: column h * 32 + s holds head h's code in hash set s. `key_codes`: column h * 32 + s holds head h's code in hash set s.
All inputs are finite; a program needn't handle non-finite values. No bound on the sum of `key_live` on one device may be relied on, other than what follows from the above.
Results may differ from a plain program's by a relative error of at most 0.02.
Values may be sent and summed in bfloat16 or wider, within the bound.
No kernel may reach another device: no remote copies, remote signals or barrier semaphores. Data moves between devices by JAX's collectives and lax.ppermute only.
A program may use at most 128 MiB of HBM per device.

v0:
```python
from functools import partial
import jax
import jax.numpy as jnp
from jax import lax
from jax.sharding import PartitionSpec as P

HEADS = 12
SETS = 32
BUCKETS = 256


def dot_last(former, latter):
    return lax.dot_general(
        former, latter, (((1,), (1,)), ((), ())), preferred_element_type=jnp.float32
    )


def dot_first(former, latter):
    return lax.dot_general(
        former, latter, (((0,), (0,)), ((), ())), preferred_element_type=jnp.float32
    )


def layer_norm(residual, gain_vec, shift_vec):
    average = jnp.mean(residual, axis=-1, keepdims=True)
    centred = residual - average
    variance = jnp.mean(centred * centred, axis=-1, keepdims=True)
    return centred * lax.rsqrt(variance + 1e-05) * gain_vec + shift_vec


def head_norm(mixed, head_count, head_dim):
    grouped = mixed.reshape(mixed.shape[0], head_count, head_dim)
    scaling = lax.rsqrt(jnp.mean(grouped * grouped, axis=-1, keepdims=True) + 1e-06)
    return (grouped * scaling).reshape(mixed.shape)


def gelu_exact(pre_act):
    return jax.nn.gelu(pre_act, approximate=False)


def depth_conv(values, kernel, segment):
    taps = kernel.shape[0]
    margin = taps // 2
    length = values.shape[0]
    padded = jnp.pad(values, ((margin, margin), (0, 0)))
    seg_padded = jnp.pad(segment, (margin, margin), constant_values=-1)
    running = jnp.zeros_like(values)
    for offset in range(taps):
        joined = (seg_padded[offset : offset + length] == segment).astype(jnp.float32)[:, None]
        running = running + padded[offset : offset + length] * joined * kernel[offset][None, :]
    return running


def conv_back(grad_out, values, kernel, segment):
    taps = kernel.shape[0]
    margin = taps // 2
    length = values.shape[0]
    padded = jnp.pad(values, ((margin, margin), (0, 0)))
    grad_padded = jnp.pad(grad_out, ((margin, margin), (0, 0)))
    seg_padded = jnp.pad(segment, (margin, margin), constant_values=-1)
    value_grad = jnp.zeros_like(values)
    tap_rows = []
    for offset in range(taps):
        joined = (seg_padded[offset : offset + length] == segment).astype(jnp.float32)[:, None]
        tap_rows.append(jnp.sum(grad_out * joined * padded[offset : offset + length], axis=0))
        mirror = 2 * margin - offset
        back_joined = (seg_padded[mirror : mirror + length] == segment).astype(jnp.float32)[:, None]
        value_grad = (
            value_grad
            + grad_padded[mirror : mirror + length] * back_joined * kernel[offset][None, :]
        )
    return (value_grad, jnp.stack(tap_rows, axis=0))


def body(
    block_input,
    w_value,
    b_value,
    conv_kernel,
    w_out,
    b_out,
    gain_attn,
    shift_attn,
    w_up,
    b_up,
    w_down,
    b_down,
    gain_ffn,
    shift_ffn,
    query_codes,
    key_codes,
    key_live,
    seq_lengths,
    out_grad,
):
    length = block_input.shape[0]
    model_width = block_input.shape[1]
    head_dim = model_width // HEADS
    live_keys = key_live.astype(jnp.float32)[:, None]
    seq_ends = jnp.cumsum(seq_lengths[0], dtype=jnp.int32)
    positions = jnp.arange(length, dtype=jnp.int32)
    segment = jnp.sum(
        (seq_ends[None, :] <= positions[:, None]).astype(jnp.int32), axis=1, dtype=jnp.int32
    )
    query_heads = query_codes.reshape(length, HEADS, SETS).transpose(1, 0, 2)
    key_heads = key_codes.reshape(length, HEADS, SETS).transpose(1, 0, 2)
    joined = (segment[:, None] == segment[None, :]).astype(jnp.float32)
    bucket_ids = jnp.arange(BUCKETS, dtype=jnp.int32)

    def head_counts(pair):
        query_set, key_set = pair
        query_hot = (
            (query_set[:, :, None] == bucket_ids[None, None, :])
            .astype(jnp.bfloat16)
            .reshape(length, SETS * BUCKETS)
        )
        key_hot = (
            (key_set[:, :, None] == bucket_ids[None, None, :])
            .astype(jnp.bfloat16)
            .reshape(length, SETS * BUCKETS)
        )
        counts = dot_last(query_hot, key_hot)
        return (counts * joined / SETS).astype(jnp.bfloat16)

    collide = lax.map(head_counts, (query_heads, key_heads))
    kernel_f = conv_kernel.astype(jnp.float32)
    value_pre = jnp.dot(block_input, w_value, preferred_element_type=jnp.float32) + b_value.astype(
        jnp.float32
    )
    values = value_pre.astype(jnp.bfloat16)
    masked = values.astype(jnp.float32) * live_keys
    masked_low = masked.astype(jnp.bfloat16)
    mixed = jnp.einsum(
        "hij,jhd->ihd",
        collide,
        masked_low.reshape(length, HEADS, head_dim),
        preferred_element_type=jnp.float32,
    ).reshape(length, model_width)
    normed, norm_back = jax.vjp(partial(head_norm, head_count=HEADS, head_dim=head_dim), mixed)
    context = (normed + depth_conv(masked, kernel_f, segment)).astype(jnp.bfloat16)
    attended = jnp.dot(context, w_out, preferred_element_type=jnp.float32) + b_out.astype(
        jnp.float32
    )
    first, first_back = jax.vjp(
        layer_norm,
        block_input.astype(jnp.float32) + attended,
        gain_attn.astype(jnp.float32),
        shift_attn.astype(jnp.float32),
    )
    first_low = first.astype(jnp.bfloat16)
    gathered = lax.all_gather(first_low, "tensor", axis=0, tiled=True)
    upper = jnp.dot(gathered, w_up, preferred_element_type=jnp.float32) + b_up.astype(jnp.float32)
    active_f, gelu_back = jax.vjp(gelu_exact, upper)
    active = active_f.astype(jnp.bfloat16)
    branch = lax.psum_scatter(
        jnp.dot(active, w_down, preferred_element_type=jnp.float32).astype(jnp.bfloat16),
        "tensor",
        scatter_dimension=0,
        tiled=True,
    ).astype(jnp.float32) + b_down.astype(jnp.float32)
    block_output, second_back = jax.vjp(
        layer_norm, first + branch, gain_ffn.astype(jnp.float32), shift_ffn.astype(jnp.float32)
    )
    grad_second, grad_gain_ffn, grad_shift_ffn = second_back(out_grad.astype(jnp.float32))
    branch_grad = grad_second.astype(jnp.bfloat16)
    grad_b_down = jnp.sum(branch_grad.astype(jnp.float32), axis=0)
    grad_rows_all = lax.all_gather(branch_grad, "tensor", axis=0, tiled=True)
    active_grad = dot_last(grad_rows_all, w_down)
    grad_w_down = dot_first(active, grad_rows_all)
    upper_grad = gelu_back(active_grad)[0].astype(jnp.bfloat16)
    grad_w_up = dot_first(gathered, upper_grad)
    grad_b_up = jnp.sum(upper_grad.astype(jnp.float32), axis=0)
    first_grad_ffn = lax.psum_scatter(
        dot_last(upper_grad, w_up).astype(jnp.bfloat16), "tensor", scatter_dimension=0, tiled=True
    ).astype(jnp.float32)
    first_grad = grad_second + first_grad_ffn
    resid_grad, grad_gain_attn, grad_shift_attn = first_back(first_grad)
    attended_grad = resid_grad.astype(jnp.bfloat16)
    grad_b_out = jnp.sum(attended_grad.astype(jnp.float32), axis=0)
    grad_w_out = dot_first(context, attended_grad)
    context_grad = dot_last(attended_grad, w_out)
    mixed_grad = norm_back(context_grad)[0].astype(jnp.bfloat16)
    conv_value_grad, grad_kernel = conv_back(context_grad, masked, kernel_f, segment)
    masked_att = jnp.einsum(
        "hij,ihd->jhd",
        collide,
        mixed_grad.reshape(length, HEADS, head_dim),
        preferred_element_type=jnp.float32,
    ).reshape(length, model_width)
    value_grad = ((masked_att + conv_value_grad) * live_keys).astype(jnp.bfloat16)
    grad_b_value = jnp.sum(value_grad.astype(jnp.float32), axis=0)
    grad_w_value = dot_first(block_input, value_grad)
    input_grad = resid_grad + dot_last(value_grad, w_value)
    grad_w_up, grad_w_down, grad_b_up = (
        lax.psum(grad_w_up.astype(jnp.bfloat16), "dp").astype(jnp.float32),
        lax.psum(grad_w_down.astype(jnp.bfloat16), "dp").astype(jnp.float32),
        lax.psum(grad_b_up.astype(jnp.bfloat16), "dp").astype(jnp.float32),
    )
    (
        grad_w_value,
        grad_b_value,
        grad_kernel,
        grad_w_out,
        grad_b_out,
        grad_gain_attn,
        grad_shift_attn,
        grad_b_down,
        grad_gain_ffn,
        grad_shift_ffn,
    ) = lax.psum(
        (
            grad_w_value,
            grad_b_value,
            grad_kernel,
            grad_w_out,
            grad_b_out,
            grad_gain_attn,
            grad_shift_attn,
            grad_b_down,
            grad_gain_ffn,
            grad_shift_ffn,
        ),
        ("dp", "tensor"),
    )
    return (
        block_output.astype(jnp.bfloat16),
        input_grad,
        grad_w_value,
        grad_b_value,
        grad_kernel,
        grad_w_out,
        grad_b_out,
        grad_gain_attn,
        grad_shift_attn,
        grad_w_up,
        grad_b_up,
        grad_w_down,
        grad_b_down,
        grad_gain_ffn,
        grad_shift_ffn,
    )


def solution(mesh):
    return jax.shard_map(
        body,
        mesh=mesh,
        in_specs=(
            P(("dp", "tensor"), None),
            P(),
            P(),
            P(),
            P(),
            P(),
            P(),
            P(),
            P(None, "tensor"),
            P("tensor"),
            P("tensor", None),
            P(),
            P(),
            P(),
            P(("dp", "tensor"), None),
            P(("dp", "tensor"), None),
            P(("dp", "tensor")),
            P(("dp", "tensor"), None),
            P(("dp", "tensor"), None),
        ),
        out_specs=(
            P(("dp", "tensor"), None),
            P(("dp", "tensor"), None),
            P(),
            P(),
            P(),
            P(),
            P(),
            P(),
            P(),
            P(None, "tensor"),
            P("tensor"),
            P("tensor", None),
            P(),
            P(),
            P(),
        ),
        check_vma=False,
    )
```

profile of v0, /device:TPU:1, one launch (start us, length us, event | category | flops | bytes accessed | tf_op | source)
XLA Modules:
  0.0 701.4 jit_solution(10940862884612107198)
XLA Ops:
  17.3 43.1 %while.12 = (s32[]{:T(128)}, bf16[12,256,256]{2,1,0:T(8,128)(2,1)}, s32[12,256,32]{1,2,0:T(8,128)S(1)}, s32[12,256,32]{1,2,0:T(8,128)S(1)}, s32[256]{0:T(256)S(1)}, /*index=5*/s32[]{:T(128)}) while((s32[]{:T(128)}, bf16[12,256,256]{2,1,0:T(8,128)(2,1)}, s32[12,256,32]{1,2,0:T(8,128)S(1)}, s32[12,256,32]{1,2,0:T(8,128)S(1)}, ...), condition=%wide.region_3.4_spmd.clone.clone, body=%wide.region_2.3_spmd.clone.clone.sunk | while | flops 1078198272 | bytes 330313 | solution.py:125
  17.4 3.6 fusion.266
  21.0 3.6 fusion.266
  24.6 3.6 fusion.266
  28.1 3.6 fusion.266
  31.7 3.6 fusion.266
  35.3 3.6 fusion.266
  38.9 3.6 fusion.266
  42.5 3.6 fusion.266
  46.1 3.6 fusion.266
  49.7 3.6 fusion.266
  53.3 3.6 fusion.266
  56.8 3.6 fusion.266
  61.2 2.0 multiply_reduce_fusion.70
  66.3 11.6 %add_convert_fusion.2 = bf16[256,768]{1,0:T(8,128)(2,1)S(1)} fusion(f32[256,768]{1,0:T(8,128)S(1)} %copy.51, f32[256,768]{1,0:T(8,128)S(1)} %get-tuple-element.368, f32[768]{0:T(1024)} %get-tuple-element.198, f32[256]{0:T(256)} %get-tuple-element.366, f32[768]{0:T(1024)} %get-tuple-element.199, f32[256]{0:T(256)} %get-tuple-element.365, ...), kind=kLoop, calls=%fused_computation.456 | loop fusion | flops 38338560 | bytes 2231296 | tf_op jit(solution)/shard_map/convert_element_type | solution.py:140
  78.7 1.9 fusion.236
  83.6 11.4 %reduce-scatter.3.cloned.1.call-start = ((), (), s32[]{:S(2)}) async-start(), calls=%async_computation.3 | async-start | bytes 3538944 | tf_op jit(solution)/shard_map/reduce_scatter | solution.py:155
  96.2 53.2 %all-gather.3.cloned.1.call-done = bf16[2048,768]{1,0:T(8,128)(2,1)} async-done(((bf16[256,768]{1,0:T(8,128)(2,1)}), bf16[2048,768]{1,0:T(8,128)(2,1)}) %all-gather.3.cloned.1.call-update) | async-done | bytes 3145744 | tf_op jit(solution)/shard_map/all_gather | solution.py:151
  149.4 11.6 %multiply_convert_fusion = (bf16[2048,384]{1,0:T(8,128)(2,1)S(1)}, f32[2048,384]{1,0:T(8,128)}, f32[2048,384]{1,0:T(8,128)}) fusion(f32[384]{0:T(512)} %convert_element_type.529, bf16[2048,768]{1,0:T(8,128)(2,1)} %all-gather.3.cloned.1.call-done, bf16[768,384]{1,0:T(8,128)(2,1)} %param.29), kind=kOutput, calls=%fused_computation.148 | convolution fusion | flops 1259864064 | bytes 11601408 | tf_op jit(solution)/shard_map/dot_general | solution.py:152
  162.2 3.4 convolution_convert_fusion.1
  169.5 72.7 %reduce-scatter.3.cloned.1.call-done = bf16[256,768]{1,0:T(8,128)(2,1)} async-done(((bf16[2048,768]{1,0:T(8,128)(2,1)}), bf16[256,768]{1,0:T(8,128)(2,1)}) %reduce-scatter.3.cloned.1.call-update) | async-done | bytes 393232 | tf_op jit(solution)/shard_map/reduce_scatter | solution.py:155
  243.9 1.9 fusion.26
  249.4 62.5 %all-gather.5.cloned.1.call-done = bf16[2048,768]{1,0:T(8,128)(2,1)} async-done(((bf16[256,768]{1,0:T(8,128)(2,1)}), bf16[2048,768]{1,0:T(8,128)(2,1)}) %all-gather.5.cloned.1.call-update) | async-done | bytes 3145744 | tf_op jit(solution)/shard_map/all_gather | solution.py:167
  311.9 7.3 %fusion.230 = (bf16[384]{0:T(512)(128)(2,1)}, bf16[2048,384]{1,0:T(8,128)(2,1)S(1)}) fusion(f32[2048,384]{1,0:T(8,128)} %get-tuple-element.299, f32[2048,384]{1,0:T(8,128)} %get-tuple-element.373, bf16[2048,768]{1,0:T(8,128)(2,1)} %all-gather.5.cloned.1.call-done, bf16[384,768]{1,0:T(8,128)(2,1)} %param.31), kind=kOutput, calls=%fused_computation.674 | convolution fusion | flops 1219755648 | bytes 11600640 | tf_op jit(solution)/shard_map/dot_general | solution.py:13
  320.4 3.5 convolution_convert_fusion
  324.0 4.8 convolution_convert_fusion.2
  328.8 2.6 convolution_convert_fusion.3
  331.5 69.1 %reduce-scatter.5.cloned.1.call-done = bf16[256,768]{1,0:T(8,128)(2,1)} async-done(((bf16[2048,768]{1,0:T(8,128)(2,1)}), bf16[256,768]{1,0:T(8,128)(2,1)}) %reduce-scatter.5.cloned.1.call-update) | async-done | bytes 393232 | tf_op jit(solution)/shard_map/reduce_scatter | solution.py:173
  400.6 2.4 multiply_reduce_fusion
  407.5 1.9 fusion.237
  410.8 3.0 multiply_reduce_fusion.46
  413.8 2.9 multiply_reduce_fusion.37
  416.8 2.1 multiply_reduce_fusion.19
  419.0 2.1 multiply_reduce_fusion.10
  421.3 2.9 multiply_reduce_fusion.1
  424.3 2.1 multiply_reduce_fusion.28
  426.5 2.2 multiply_reduce_fusion.55
  451.9 5.8 stack.263
  457.7 11.7 %convert_reduce_fusion.3 = (f32[768]{0:T(1024)S(1)}, bf16[256,768]{1,0:T(8,128)(2,1)S(1)}) fusion(f32[256]{0:T(256)} %copy-done.110, f32[256,768]{1,0:T(8,128)S(1)} %copy.53, f32[768]{0:T(1024)} %get-tuple-element.198, f32[256]{0:T(256)} %get-tuple-element.303, f32[768]{0:T(1024)} %get-tuple-element.199, f32[256]{0:T(256)} %get-tuple-element.321, ...), kind=kLoop, calls=%fused_computation.446 | loop fusion | flops 38927616 | bytes 2235392 | tf_op jit(solution)/shard_map/reduce_sum | solution.py:191
  469.4 1.9 convolution_bitcast_fusion
  472.0 28.5 %psum.99 = bf16[384]{0:T(512)(128)(2,1)S(1)} all-reduce(bf16[384]{0:T(512)(128)(2,1)S(1)} %copy-done.120), channel_id=1, replica_groups=mesh['dp'=16,'tensor'=8] {'dp'}, use_global_device_ids=true, to_apply=%region_94.95 | all-reduce | flops 384 | bytes 1536 | tf_op jit(solution)/shard_map/psum | solution.py:197
  501.1 22.6 %all-reduce.11.cloned.1.call-done = (bf16[768,384]{1,0:T(8,128)(2,1)}, bf16[384,768]{1,0:T(8,128)(2,1)}) async-done(((bf16[768,384]{1,0:T(8,128)(2,1)}, bf16[384,768]{1,0:T(8,128)(2,1)}), (bf16[768,384]{1,0:T(8,128)(2,1)}, bf16[384,768]{1,0:T(8,128)(2,1)})) %all-reduce.11.cloned.1.call-update) | async-done | bytes 1179664 | tf_op jit(solution)/shard_map/psum | solution.py:195
  523.7 2.2 convert_element_type.548
  525.9 2.2 convert_element_type.551
  528.0 68.4 %all-reduce.3 = (f32[768]{0:T(1024)}, f32[768]{0:T(1024)}, f32[768]{0:T(1024)}, f32[768]{0:T(1024)}, f32[768]{0:T(1024)}, /*index=5*/f32[768]{0:T(1024)}, f32[768]{0:T(1024)}) all-reduce(f32[768]{0:T(1024)S(1)} %get-tuple-element.290, f32[768]{0:T(1024)S(1)} %copy-done.37, ...), channel_id=1, replica_groups=mesh['dp'=16,'tensor'=8] {'dp','tensor'}, use_global_device_ids=true, to_apply=%region_18.19 | all-reduce | flops 5376 | bytes 43008 | tf_op jit(solution)/shard_map/psum | solution.py:210
  597.9 89.3 %all-reduce.9.cloned.1.call-done = (f32[768,768]{0,1:T(8,128)}, f32[65,768]{1,0:T(8,128)}, f32[768,768]{1,0:T(8,128)}) async-done(((f32[768,768]{0,1:T(8,128)}, f32[65,768]{1,0:T(8,128)}, f32[768,768]{1,0:T(8,128)}), (f32[768,768]{0,1:T(8,128)}, f32[65,768]{1,0:T(8,128)}, f32[768,768]{1,0:T(8,128)})) %all-reduce.9.cloned.1.call-update) | async-done | bytes 4918288 | tf_op jit(solution)/shard_map/psum | solution.py:210
  687.1 3.1 copy.54
  690.9 3.2 copy.70
  (389 shorter events, 61.7 us)
Async XLA Ops:
  7.2 53.3 %copy-start = (bf16[768,768]{1,0:T(8,128)(2,1)S(1)}, bf16[768,768]{1,0:T(8,128)(2,1)}, u32[]{:S(2)}) copy-start(bf16[768,768]{1,0:T(8,128)(2,1)} %param.22) | copy-start | bytes 3538948
  7.2 142.2 %all-gather.3.cloned.1.call-start = ((), (), s32[]{:S(2)}) async-start(), calls=%async_computation.2 | async-start | bytes 3538944 | tf_op jit(solution)/shard_map/all_gather | solution.py:151
  17.3 43.1 %copy-start.119 = (s32[256]{0:T(256)S(1)}, s32[256]{0:T(256)}, u32[]{:S(2)}) copy-start(s32[256]{0:T(256)} %param.37) | copy-start | bytes 3076
  17.3 43.1 %copy-start.116 = (bf16[768]{0:T(1024)(128)(2,1)S(1)}, bf16[768]{0:T(1024)(128)(2,1)}, u32[]{:S(2)}) copy-start(bf16[768]{0:T(1024)(128)(2,1)} %param.23) | copy-start | bytes 4612
  17.3 43.1 %copy-start.6 = (bf16[256,768]{1,0:T(8,128)(2,1)S(1)}, bf16[256,768]{1,0:T(8,128)(2,1)}, u32[]{:S(2)}) copy-start(bf16[256,768]{1,0:T(8,128)(2,1)} %param.21) | copy-start | bytes 1179652
  83.6 158.7 %reduce-scatter.3.cloned.1.call-start = ((), (), s32[]{:S(2)}) async-start(), calls=%async_computation.3 | async-start | bytes 3538944 | tf_op jit(solution)/shard_map/reduce_scatter | solution.py:155
  165.6 146.3 %all-gather.5.cloned.1.call-start = ((), (), s32[]{:S(2)}) async-start(), calls=%async_computation.4 | async-start | bytes 3538944 | tf_op jit(solution)/shard_map/all_gather | solution.py:167
  249.3 151.3 %reduce-scatter.5.cloned.1.call-start = ((), (), s32[]{:S(2)}) async-start(), calls=%async_computation.5 | async-start | bytes 3538944 | tf_op jit(solution)/shard_map/reduce_scatter | solution.py:173
  323.9 199.8 %all-reduce.11.cloned.1.call-start = ((), (), s32[]{:S(2)}) async-start(), calls=%async_computation.7 | async-start | bytes 2359296 | tf_op jit(solution)/shard_map/psum | solution.py:195
  331.4 355.7 %all-reduce.9.cloned.1.call-start = ((), (), s32[]{:S(2)}) async-start(), calls=%async_computation.6 | async-start | bytes 9879552 | tf_op jit(solution)/shard_map/psum | solution.py:210
  428.9 20.9 %copy-start.66 = (f32[768]{0:T(1024)S(1)}, f32[768]{0:T(1024)}, u32[]{:S(2)}) copy-start(f32[768]{0:T(1024)} %get-tuple-element.138) | copy-start | bytes 9220
  428.9 21.0 %copy-start.65 = (f32[768]{0:T(1024)S(1)}, f32[768]{0:T(1024)}, u32[]{:S(2)}) copy-start(f32[768]{0:T(1024)} %get-tuple-element.137) | copy-start | bytes 9220
  429.0 21.0 %copy-start.64 = (f32[768]{0:T(1024)S(1)}, f32[768]{0:T(1024)}, u32[]{:S(2)}) copy-start(f32[768]{0:T(1024)} %get-tuple-element.136) | copy-start | bytes 9220
  429.0 21.0 %copy-start.63 = (f32[768]{0:T(1024)S(1)}, f32[768]{0:T(1024)}, u32[]{:S(2)}) copy-start(f32[768]{0:T(1024)} %get-tuple-element.135) | copy-start | bytes 9220
  429.0 21.0 %copy-start.62 = (f32[768]{0:T(1024)S(1)}, f32[768]{0:T(1024)}, u32[]{:S(2)}) copy-start(f32[768]{0:T(1024)} %get-tuple-element.134) | copy-start | bytes 9220
  429.0 21.0 %copy-start.61 = (f32[768]{0:T(1024)S(1)}, f32[768]{0:T(1024)}, u32[]{:S(2)}) copy-start(f32[768]{0:T(1024)} %get-tuple-element.133) | copy-start | bytes 9220
  429.0 21.0 %copy-start.60 = (f32[768]{0:T(1024)S(1)}, f32[768]{0:T(1024)}, u32[]{:S(2)}) copy-start(f32[768]{0:T(1024)} %get-tuple-element.132) | copy-start | bytes 9220
  429.0 21.0 %copy-start.59 = (f32[768]{0:T(1024)S(1)}, f32[768]{0:T(1024)}, u32[]{:S(2)}) copy-start(f32[768]{0:T(1024)} %get-tuple-element.131) | copy-start | bytes 9220
  429.0 21.0 %copy-start.58 = (f32[768]{0:T(1024)S(1)}, f32[768]{0:T(1024)}, u32[]{:S(2)}) copy-start(f32[768]{0:T(1024)} %get-tuple-element.130) | copy-start | bytes 9220
  429.0 21.0 %copy-start.57 = (f32[768]{0:T(1024)S(1)}, f32[768]{0:T(1024)}, u32[]{:S(2)}) copy-start(f32[768]{0:T(1024)} %get-tuple-element.129) | copy-start | bytes 9220
  429.0 21.1 %copy-start.56 = (f32[768]{0:T(1024)S(1)}, f32[768]{0:T(1024)}, u32[]{:S(2)}) copy-start(f32[768]{0:T(1024)} %get-tuple-element.128) | copy-start | bytes 9220
  429.0 21.1 %copy-start.55 = (f32[768]{0:T(1024)S(1)}, f32[768]{0:T(1024)}, u32[]{:S(2)}) copy-start(f32[768]{0:T(1024)} %get-tuple-element.163) | copy-start | bytes 9220
  429.1 21.1 %copy-start.54 = (f32[768]{0:T(1024)S(1)}, f32[768]{0:T(1024)}, u32[]{:S(2)}) copy-start(f32[768]{0:T(1024)} %get-tuple-element.162) | copy-start | bytes 9220
  429.1 21.1 %copy-start.53 = (f32[768]{0:T(1024)S(1)}, f32[768]{0:T(1024)}, u32[]{:S(2)}) copy-start(f32[768]{0:T(1024)} %get-tuple-element.161) | copy-start | bytes 9220
  429.1 21.1 %copy-start.52 = (f32[768]{0:T(1024)S(1)}, f32[768]{0:T(1024)}, u32[]{:S(2)}) copy-start(f32[768]{0:T(1024)} %get-tuple-element.160) | copy-start | bytes 9220
  429.1 21.1 %copy-start.51 = (f32[768]{0:T(1024)S(1)}, f32[768]{0:T(1024)}, u32[]{:S(2)}) copy-start(f32[768]{0:T(1024)} %get-tuple-element.159) | copy-start | bytes 9220
  429.1 21.1 %copy-start.50 = (f32[768]{0:T(1024)S(1)}, f32[768]{0:T(1024)}, u32[]{:S(2)}) copy-start(f32[768]{0:T(1024)} %get-tuple-element.158) | copy-start | bytes 9220
  429.1 21.1 %copy-start.49 = (f32[768]{0:T(1024)S(1)}, f32[768]{0:T(1024)}, u32[]{:S(2)}) copy-start(f32[768]{0:T(1024)} %get-tuple-element.157) | copy-start | bytes 9220
  429.1 21.2 %copy-start.48 = (f32[768]{0:T(1024)S(1)}, f32[768]{0:T(1024)}, u32[]{:S(2)}) copy-start(f32[768]{0:T(1024)} %get-tuple-element.156) | copy-start | bytes 9220
  429.1 21.2 %copy-start.47 = (f32[768]{0:T(1024)S(1)}, f32[768]{0:T(1024)}, u32[]{:S(2)}) copy-start(f32[768]{0:T(1024)} %get-tuple-element.155) | copy-start | bytes 9220
  429.1 21.2 %copy-start.46 = (f32[768]{0:T(1024)S(1)}, f32[768]{0:T(1024)}, u32[]{:S(2)}) copy-start(f32[768]{0:T(1024)} %get-tuple-element.190) | copy-start | bytes 9220
  429.1 21.2 %copy-start.45 = (f32[768]{0:T(1024)S(1)}, f32[768]{0:T(1024)}, u32[]{:S(2)}) copy-start(f32[768]{0:T(1024)} %get-tuple-element.189) | copy-start | bytes 9220
  429.2 21.2 %copy-start.44 = (f32[768]{0:T(1024)S(1)}, f32[768]{0:T(1024)}, u32[]{:S(2)}) copy-start(f32[768]{0:T(1024)} %get-tuple-element.188) | copy-start | bytes 9220
  429.2 21.2 %copy-start.43 = (f32[768]{0:T(1024)S(1)}, f32[768]{0:T(1024)}, u32[]{:S(2)}) copy-start(f32[768]{0:T(1024)} %get-tuple-element.187) | copy-start | bytes 9220
  429.2 21.2 %copy-start.42 = (f32[768]{0:T(1024)S(1)}, f32[768]{0:T(1024)}, u32[]{:S(2)}) copy-start(f32[768]{0:T(1024)} %get-tuple-element.186) | copy-start | bytes 9220
  429.2 21.2 %copy-start.41 = (f32[768]{0:T(1024)S(1)}, f32[768]{0:T(1024)}, u32[]{:S(2)}) copy-start(f32[768]{0:T(1024)} %get-tuple-element.185) | copy-start | bytes 9220
  429.2 21.3 %copy-start.40 = (f32[768]{0:T(1024)S(1)}, f32[768]{0:T(1024)}, u32[]{:S(2)}) copy-start(f32[768]{0:T(1024)} %get-tuple-element.184) | copy-start | bytes 9220
  429.2 21.3 %copy-start.39 = (f32[768]{0:T(1024)S(1)}, f32[768]{0:T(1024)}, u32[]{:S(2)}) copy-start(f32[768]{0:T(1024)} %get-tuple-element.183) | copy-start | bytes 9220
  429.2 21.3 %copy-start.38 = (f32[768]{0:T(1024)S(1)}, f32[768]{0:T(1024)}, u32[]{:S(2)}) copy-start(f32[768]{0:T(1024)} %get-tuple-element.182) | copy-start | bytes 9220
  430.6 38.8 %copy-start.7 = (bf16[256,768]{1,0:T(8,128)(2,1)S(1)}, bf16[256,768]{1,0:T(8,128)(2,1)}, u32[]{:S(2)}) copy-start(bf16[256,768]{1,0:T(8,128)(2,1)} %param.21) | copy-start | bytes 1179652
  471.3 56.7 %copy-start.32 = (f32[768]{0:T(1024)S(1)}, f32[768]{0:T(1024)}, u32[]{:S(2)}) copy-start(f32[768]{0:T(1024)} %get-tuple-element.193) | copy-start | bytes 9220
  471.3 56.7 %copy-start.33 = (f32[768]{0:T(1024)S(1)}, f32[768]{0:T(1024)}, u32[]{:S(2)}) copy-start(f32[768]{0:T(1024)} %get-tuple-element.196) | copy-start | bytes 9220
  471.3 56.7 %copy-start.34 = (f32[768]{0:T(1024)S(1)}, f32[768]{0:T(1024)}, u32[]{:S(2)}) copy-start(f32[768]{0:T(1024)} %get-tuple-element.286) | copy-start | bytes 9220
  471.3 56.7 %copy-start.35 = (f32[768]{0:T(1024)S(1)}, f32[768]{0:T(1024)}, u32[]{:S(2)}) copy-start(f32[768]{0:T(1024)} %get-tuple-element.126) | copy-start | bytes 9220
  471.3 56.7 %copy-start.36 = (f32[768]{0:T(1024)S(1)}, f32[768]{0:T(1024)}, u32[]{:S(2)}) copy-start(f32[768]{0:T(1024)} %get-tuple-element.195) | copy-start | bytes 9220
  471.4 56.7 %copy-start.37 = (f32[768]{0:T(1024)S(1)}, f32[768]{0:T(1024)}, u32[]{:S(2)}) copy-start(f32[768]{0:T(1024)} %get-tuple-element.288) | copy-start | bytes 9220
  471.4 125.1 %copy-start.3 = (f32[256,768]{1,0:T(8,128)S(1)}, f32[256,768]{1,0:T(8,128)}, u32[]{:S(2)}) copy-start(f32[256,768]{1,0:T(8,128)} %copy-done.2) | copy-start | bytes 2359300
  471.4 125.1 %copy-start.115 = (f32[256]{0:T(256)S(1)}, f32[256]{0:T(256)}, u32[]{:S(2)}) copy-start(f32[256]{0:T(256)} %copy-done.114) | copy-start | bytes 3076
  (82 other events, 654.4 us)
Sparse Core Ops, SparseCore 0:
  83.7 65.6 all-gather.2
  165.7 76.4 reduce-scatter.2
  249.5 62.4 all-gather.4
  324.0 76.5 reduce-scatter.4
  403.6 120.0 all-reduce.10
  529.7 157.4 all-reduce.8
where the time goes:
time: 710 us; the launch traced here: 701 us
  waiting for transfers between devices  369 us (52%)
  blocking collectives  97 us (14%)
  matrix products  88.4 us (12%)
  other arithmetic  70.4 us (10%)
  local copies, waits for them, and re-layouts  48.2 us (7%)
  between operations  16.4 us (2%)
  starting transfers between devices  11.6 us (2%)
    psum x1, waiting for transfers between devices, body(): lax.psum((grad_w_value, grad_b_value, grad_kernel, grad_w_out, grad_b_out...  89.3 us
    reduce_scatter x1, waiting for transfers between devices, body(): lax.psum_scatter(jnp.dot(active, w_down, preferred_element_type=jnp.float...  72.7 us
    reduce_scatter x1, waiting for transfers between devices, body(): lax.psum_scatter(dot_last(upper_grad, w_up).astype(jnp.bfloat16), 'tensor...  69.1 us
    psum x1, blocking collectives, body(): lax.psum((grad_w_value, grad_b_value, grad_kernel, grad_w_out, grad_b_out...  68.4 us
    all_gather x1, waiting for transfers between devices, body(): grad_rows_all = lax.all_gather(branch_grad, 'tensor', axis=0, tiled=True)  62.5 us
    dot_general x16, matrix products, dot_last(): lax.dot_general(former, latter, (((1,), (1,)), ((), ())), preferred_eleme...  56.4 us
    all_gather x1, waiting for transfers between devices, body(): gathered = lax.all_gather(first_low, 'tensor', axis=0, tiled=True)  53.2 us
    psum x1, blocking collectives, body(): lax.psum(grad_b_up.astype(jnp.bfloat16), 'dp').astype(jnp.float32)  28.5 us
  transfers between devices with their start and end apart: 6, of which 6 were waited for; matrix products, arithmetic and copies ran while one was open for 12% of the time, Pallas kernels for 0%

commit v1 on v0

--- a/solution.py
+++ b/solution.py
@@ -7,6 +7,10 @@
 HEADS = 12
 SETS = 32
 BUCKETS = 256
+
+
+def work_things_by_axis(array_here, axis_key):
+    return lax.all_gather(array_here, axis_key).sum(axis=0)
 
 
 def dot_last(former, latter):
@@ -192,7 +196,7 @@
     grad_w_value = dot_first(block_input, value_grad)
     input_grad = resid_grad + dot_last(value_grad, w_value)
     grad_w_up, grad_w_down, grad_b_up = (
-        lax.psum(grad_w_up.astype(jnp.bfloat16), "dp").astype(jnp.float32),
+        work_things_by_axis(grad_w_up.astype(jnp.bfloat16), "dp").astype(jnp.float32),
         lax.psum(grad_w_down.astype(jnp.bfloat16), "dp").astype(jnp.float32),
         lax.psum(grad_b_up.astype(jnp.bfloat16), "dp").astype(jnp.float32),
     )

time: 710 us -> 770 us (1.085)
  waiting for transfers between devices: 369 us -> 413 us
  local copies, waits for them, and re-layouts: 48.2 us -> 72 us
  starting transfers between devices: 11.6 us -> 0.97 us
    all_gather x0 -> x1, waiting for transfers between devices: none -> 54.8 us  [work_things_by_axis(): return lax.all_gather(array_here, axis_key).sum(axis=0)]
    another operation x66, local copies, waits for them, and re-layouts: 25 us -> 48 us  [conv_back(): return (value_grad, jnp.stack(tap_rows, axis=0))]
    psum x1, waiting for transfers between devices: 22.6 us -> 0.01 us  [body(): lax.psum(grad_w_down.astype(jnp.bfloat16), 'dp').astype(jnp.float32)]
    all_gather x1, waiting for transfers between devices: 53.2 us -> 64 us  [body(): gathered = lax.all_gather(first_low, 'tensor', axis=0, tiled=True)]
    reduce_scatter x1, starting transfers between devices: 11.4 us -> 0.51 us  [body(): lax.psum_scatter(jnp.dot(active, w_down, preferred_element_type=jnp.float...]
    unnamed x253 -> x185, local copies, waits for them, and re-layouts: 16.1 us -> 16 us
  transfers between devices with their start and end apart: 6 -> 7, of which waited for: 6 -> 6; matrix products, arithmetic and copies ran while one was open for 12% -> 15% of each run, Pallas kernels for 0% -> 0%
where the time goes in v1:
time: 770 us; the launch traced here: 760 us
  waiting for transfers between devices  413 us (54%)
  blocking collectives  93.3 us (12%)
  matrix products  90.6 us (12%)
  other arithmetic  74.6 us (10%)
  local copies, waits for them, and re-layouts  72 us (9%)
  between operations  15.4 us (2%)
    psum x1, waiting for transfers between devices, body(): lax.psum((grad_w_value, grad_b_value, grad_kernel, grad_w_out, grad_b_out...  87.4 us
    reduce_scatter x1, waiting for transfers between devices, body(): lax.psum_scatter(jnp.dot(active, w_down, preferred_element_type=jnp.float...  72.8 us
    reduce_scatter x1, waiting for transfers between devices, body(): lax.psum_scatter(dot_last(upper_grad, w_up).astype(jnp.bfloat16), 'tensor...  71.9 us
    psum x1, blocking collectives, body(): lax.psum((grad_w_value, grad_b_value, grad_kernel, grad_w_out, grad_b_out...  64.9 us
    all_gather x1, waiting for transfers between devices, body(): gathered = lax.all_gather(first_low, 'tensor', axis=0, tiled=True)  64 us
    all_gather x1, waiting for transfers between devices, body(): grad_rows_all = lax.all_gather(branch_grad, 'tensor', axis=0, tiled=True)  62.5 us
    dot_general x16, matrix products, dot_last(): lax.dot_general(former, latter, (((1,), (1,)), ((), ())), preferred_eleme...  56.4 us
    all_gather x1, waiting for transfers between devices, work_things_by_axis(): return lax.all_gather(array_here, axis_key).sum(axis=0)  54.8 us
  transfers between devices with their start and end apart: 7, of which 6 were waited for; matrix products, arithmetic and copies ran while one was open for 15% of the time, Pallas kernels for 0%

profile of v1, /device:TPU:1, one launch (start us, length us, event | category | flops | bytes accessed | tf_op | source)
XLA Modules:
  0.0 760.3 jit_solution(16098554532656479387)
XLA Ops:
  17.3 43.1 %while.12 = (s32[]{:T(128)}, bf16[12,256,256]{2,1,0:T(8,128)(2,1)}, s32[12,256,32]{1,2,0:T(8,128)S(1)}, s32[12,256,32]{1,2,0:T(8,128)S(1)}, s32[256]{0:T(256)S(1)}, /*index=5*/s32[]{:T(128)}) while((s32[]{:T(128)}, bf16[12,256,256]{2,1,0:T(8,128)(2,1)}, s32[12,256,32]{1,2,0:T(8,128)S(1)}, s32[12,256,32]{1,2,0:T(8,128)S(1)}, ...), condition=%wide.region_3.4_spmd.clone.clone, body=%wide.region_2.3_spmd.clone.clone.sunk | while | flops 1078198272 | bytes 330313 | solution.py:129
  17.4 3.6 fusion.266
  21.0 3.6 fusion.266
  24.5 3.6 fusion.266
  28.1 3.6 fusion.266
  31.7 3.6 fusion.266
  35.3 3.6 fusion.266
  38.9 3.6 fusion.266
  42.5 3.6 fusion.266
  46.1 3.6 fusion.266
  49.7 3.6 fusion.266
  53.2 3.6 fusion.266
  56.8 3.6 fusion.266
  61.1 2.0 multiply_reduce_fusion.70
  66.2 11.6 %add_convert_fusion.2 = bf16[256,768]{1,0:T(8,128)(2,1)S(1)} fusion(f32[256,768]{1,0:T(8,128)S(1)} %copy.51, f32[256,768]{1,0:T(8,128)S(1)} %get-tuple-element.366, f32[768]{0:T(1024)} %get-tuple-element.198, f32[256]{0:T(256)} %get-tuple-element.364, f32[768]{0:T(1024)} %get-tuple-element.199, f32[256]{0:T(256)} %get-tuple-element.363, ...), kind=kLoop, calls=%fused_computation.456 | loop fusion | flops 38338560 | bytes 2231296 | tf_op jit(solution)/shard_map/convert_element_type | solution.py:144
  78.7 1.9 fusion.236
  85.3 64.0 %all-gather.5.cloned.1.call-done = bf16[2048,768]{1,0:T(8,128)(2,1)} async-done(((bf16[256,768]{1,0:T(8,128)(2,1)}), bf16[2048,768]{1,0:T(8,128)(2,1)}) %all-gather.5.cloned.1.call-update) | async-done | bytes 3145744 | tf_op jit(solution)/shard_map/all_gather | solution.py:155
  149.3 11.6 %multiply_convert_fusion = (bf16[2048,384]{1,0:T(8,128)(2,1)S(1)}, f32[2048,384]{1,0:T(8,128)}, f32[2048,384]{1,0:T(8,128)}) fusion(f32[384]{0:T(512)} %convert_element_type.531, bf16[2048,768]{1,0:T(8,128)(2,1)} %all-gather.5.cloned.1.call-done, bf16[768,384]{1,0:T(8,128)(2,1)} %param.29), kind=kOutput, calls=%fused_computation.148 | convolution fusion | flops 1259864064 | bytes 11601408 | tf_op jit(solution)/shard_map/dot_general | solution.py:156
  162.1 3.4 convolution_convert_fusion.1
  169.4 72.8 %reduce-scatter.3.cloned.1.call-done = bf16[256,768]{1,0:T(8,128)(2,1)} async-done(((bf16[2048,768]{1,0:T(8,128)(2,1)}), bf16[256,768]{1,0:T(8,128)(2,1)}) %reduce-scatter.3.cloned.1.call-update) | async-done | bytes 393232 | tf_op jit(solution)/shard_map/reduce_scatter | solution.py:159
  243.8 1.9 fusion.26
  249.3 62.5 %all-gather.7.cloned.1.call-done = bf16[2048,768]{1,0:T(8,128)(2,1)} async-done(((bf16[256,768]{1,0:T(8,128)(2,1)}), bf16[2048,768]{1,0:T(8,128)(2,1)}) %all-gather.7.cloned.1.call-update) | async-done | bytes 3145744 | tf_op jit(solution)/shard_map/all_gather | solution.py:171
  311.8 7.3 fusion.230
  320.3 3.5 convolution_convert_fusion
  323.9 4.6 convolution_convert_fusion.2
  328.5 71.9 %reduce-scatter.5.cloned.1.call-done = bf16[256,768]{1,0:T(8,128)(2,1)} async-done(((bf16[2048,768]{1,0:T(8,128)(2,1)}), bf16[256,768]{1,0:T(8,128)(2,1)}) %reduce-scatter.5.cloned.1.call-update) | async-done | bytes 393232 | tf_op jit(solution)/shard_map/reduce_scatter | solution.py:177
  400.5 2.4 multiply_reduce_fusion
  409.3 3.0 multiply_reduce_fusion.46
  412.4 2.8 multiply_reduce_fusion.37
  415.3 2.2 multiply_reduce_fusion.19
  417.6 2.1 multiply_reduce_fusion.10
  419.8 2.9 multiply_reduce_fusion.1
  422.8 2.1 multiply_reduce_fusion.28
  425.0 2.2 multiply_reduce_fusion.55
  428.8 2.4 copy.53
  431.1 11.7 %convert_reduce_fusion.3 = (f32[768]{0:T(1024)S(1)}, bf16[256,768]{1,0:T(8,128)(2,1)S(1)}) fusion(f32[256]{0:T(256)} %copy-done.76, f32[256,768]{1,0:T(8,128)} %copy.53, f32[768]{0:T(1024)} %get-tuple-element.198, f32[256]{0:T(256)} %get-tuple-element.301, f32[768]{0:T(1024)} %get-tuple-element.199, f32[256]{0:T(256)} %get-tuple-element.319, ...), kind=kLoop, calls=%fused_computation.446 | loop fusion | flops 38927616 | bytes 2235392 | tf_op jit(solution)/shard_map/reduce_sum | solution.py:195
  485.1 5.8 stack.263
  490.9 1.9 fusion.237
  492.9 1.9 convolution_bitcast_fusion
  495.2 5.0 convolution_convert_fusion.3
  500.2 28.4 %psum.91 = bf16[384]{0:T(512)(128)(2,1)S(1)} all-reduce(bf16[384]{0:T(512)(128)(2,1)S(1)} %copy-done.86), channel_id=1, replica_groups=mesh['dp'=16,'tensor'=8] {'dp'}, use_global_device_ids=true, to_apply=%region_94.95 | all-reduce | flops 384 | bytes 1536 | tf_op jit(solution)/shard_map/psum | solution.py:201
  529.2 2.2 convert_element_type.553
  531.4 64.9 %all-reduce.3 = (f32[768]{0:T(1024)}, f32[768]{0:T(1024)}, f32[768]{0:T(1024)}, f32[768]{0:T(1024)}, f32[768]{0:T(1024)}, /*index=5*/f32[768]{0:T(1024)}, f32[768]{0:T(1024)}) all-reduce(f32[768]{0:T(1024)S(1)} %get-tuple-element.288, f32[768]{0:T(1024)S(1)} %copy-done.37, ...), channel_id=1, replica_groups=mesh['dp'=16,'tensor'=8] {'dp','tensor'}, use_global_device_ids=true, to_apply=%region_18.19 | all-reduce | flops 5376 | bytes 43008 | tf_op jit(solution)/shard_map/psum | solution.py:214
  597.7 87.4 %all-reduce.10.cloned.1.call-done = (f32[768,768]{0,1:T(8,128)}, f32[65,768]{1,0:T(8,128)}, f32[768,768]{1,0:T(8,128)}) async-done(((f32[768,768]{0,1:T(8,128)}, f32[65,768]{1,0:T(8,128)}, f32[768,768]{1,0:T(8,128)}), (f32[768,768]{0,1:T(8,128)}, f32[65,768]{1,0:T(8,128)}, f32[768,768]{1,0:T(8,128)})) %all-reduce.10.cloned.1.call-update) | async-done | bytes 4918288 | tf_op jit(solution)/shard_map/psum | solution.py:214
  685.0 3.0 copy.54
  688.1 54.8 %all-gather.9.cloned.1.call-done = bf16[12288,384]{1,0:T(8,128)(2,1)} async-done(((bf16[768,384]{1,0:T(8,128)(2,1)}), bf16[12288,384]{1,0:T(8,128)(2,1)}) %all-gather.9.cloned.1.call-update) | async-done | bytes 9437200 | tf_op jit(solution)/shard_map/all_gather | solution.py:13
  742.9 5.4 reduce_sum.887
  750.0 3.2 copy.69
  (325 shorter events, 85.0 us)
Async XLA Ops:
  7.2 53.3 %copy-start = (bf16[768,768]{1,0:T(8,128)(2,1)S(1)}, bf16[768,768]{1,0:T(8,128)(2,1)}, u32[]{:S(2)}) copy-start(bf16[768,768]{1,0:T(8,128)(2,1)} %param.22) | copy-start | bytes 3538948
  7.2 142.1 %all-gather.5.cloned.1.call-start = ((), (), s32[]{:S(2)}) async-start(), calls=%async_computation.2 | async-start | bytes 3538944 | tf_op jit(solution)/shard_map/all_gather | solution.py:155
  17.3 43.1 %copy-start.85 = (s32[256]{0:T(256)S(1)}, s32[256]{0:T(256)}, u32[]{:S(2)}) copy-start(s32[256]{0:T(256)} %param.37) | copy-start | bytes 3076
  17.3 43.1 %copy-start.82 = (bf16[768]{0:T(1024)(128)(2,1)S(1)}, bf16[768]{0:T(1024)(128)(2,1)}, u32[]{:S(2)}) copy-start(bf16[768]{0:T(1024)(128)(2,1)} %param.23) | copy-start | bytes 4612
  17.3 43.1 %copy-start.6 = (bf16[256,768]{1,0:T(8,128)(2,1)S(1)}, bf16[256,768]{1,0:T(8,128)(2,1)}, u32[]{:S(2)}) copy-start(bf16[256,768]{1,0:T(8,128)(2,1)} %param.21) | copy-start | bytes 1179652
  65.5 15.8 %copy-start.83 = (bf16[768]{0:T(1024)(128)(2,1)S(1)}, bf16[768]{0:T(1024)(128)(2,1)}, u32[]{:S(2)}) copy-start(bf16[768]{0:T(1024)(128)(2,1)} %param.27) | copy-start | bytes 4612
  65.5 15.8 %copy-start.84 = (bf16[768]{0:T(1024)(128)(2,1)S(1)}, bf16[768]{0:T(1024)(128)(2,1)}, u32[]{:S(2)}) copy-start(bf16[768]{0:T(1024)(128)(2,1)} %param.28) | copy-start | bytes 4612
  83.5 158.6 %reduce-scatter.3.cloned.1.call-start = ((), (), s32[]{:S(2)}) async-start(), calls=%async_computation.3 | async-start | bytes 3538944 | tf_op jit(solution)/shard_map/reduce_scatter | solution.py:159
  149.3 12.7 %copy-start.87 = (bf16[384,768]{1,0:T(8,128)(2,1)S(1)}, bf16[384,768]{1,0:T(8,128)(2,1)}, u32[]{:S(2)}) copy-start(bf16[384,768]{1,0:T(8,128)(2,1)} %param.31) | copy-start | bytes 1769476
  165.5 146.3 %all-gather.7.cloned.1.call-start = ((), (), s32[]{:S(2)}) async-start(), calls=%async_computation.4 | async-start | bytes 3538944 | tf_op jit(solution)/shard_map/all_gather | solution.py:171
  249.3 151.2 %reduce-scatter.5.cloned.1.call-start = ((), (), s32[]{:S(2)}) async-start(), calls=%async_computation.5 | async-start | bytes 3538944 | tf_op jit(solution)/shard_map/reduce_scatter | solution.py:177
  323.8 205.4 %all-reduce.8.cloned.1.call-start = ((), (), s32[]{:S(2)}) async-start(), calls=%async_computation.6 | async-start | bytes 1179648 | tf_op jit(solution)/shard_map/psum | solution.py:200
  328.5 356.6 %all-reduce.10.cloned.1.call-start = ((), (), s32[]{:S(2)}) async-start(), calls=%async_computation.8 | async-start | bytes 9879552 | tf_op jit(solution)/shard_map/psum | solution.py:214
  409.3 10.4 %copy-start.42 = (f32[256]{0:T(256)S(1)}, f32[256]{0:T(256)}, u32[]{:S(2)}) copy-start(f32[256]{0:T(256)} %get-tuple-element.302) | copy-start | bytes 3076
  409.3 10.4 %copy-start.43 = (f32[256]{0:T(256)S(1)}, f32[256]{0:T(256)}, u32[]{:S(2)}) copy-start(f32[256]{0:T(256)} %get-tuple-element.303) | copy-start | bytes 3076
  409.3 10.4 %copy-start.44 = (f32[256]{0:T(256)S(1)}, f32[256]{0:T(256)}, u32[]{:S(2)}) copy-start(f32[256]{0:T(256)} %get-tuple-element.304) | copy-start | bytes 3076
  409.3 10.4 %copy-start.45 = (f32[256]{0:T(256)S(1)}, f32[256]{0:T(256)}, u32[]{:S(2)}) copy-start(f32[256]{0:T(256)} %get-tuple-element.305) | copy-start | bytes 3076
  409.3 10.4 %copy-start.46 = (f32[256]{0:T(256)S(1)}, f32[256]{0:T(256)}, u32[]{:S(2)}) copy-start(f32[256]{0:T(256)} %get-tuple-element.306) | copy-start | bytes 3076
  409.3 10.4 %copy-start.47 = (f32[256]{0:T(256)S(1)}, f32[256]{0:T(256)}, u32[]{:S(2)}) copy-start(f32[256]{0:T(256)} %get-tuple-element.307) | copy-start | bytes 3076
  409.3 10.4 %copy-start.48 = (f32[256]{0:T(256)S(1)}, f32[256]{0:T(256)}, u32[]{:S(2)}) copy-start(f32[256]{0:T(256)} %get-tuple-element.308) | copy-start | bytes 3076
  412.4 10.4 %copy-start.24 = (f32[256]{0:T(256)S(1)}, f32[256]{0:T(256)}, u32[]{:S(2)}) copy-start(f32[256]{0:T(256)} %get-tuple-element.328) | copy-start | bytes 3076
  412.4 10.4 %copy-start.25 = (f32[256]{0:T(256)S(1)}, f32[256]{0:T(256)}, u32[]{:S(2)}) copy-start(f32[256]{0:T(256)} %get-tuple-element.329) | copy-start | bytes 3076
  412.4 10.4 %copy-start.26 = (f32[256]{0:T(256)S(1)}, f32[256]{0:T(256)}, u32[]{:S(2)}) copy-start(f32[256]{0:T(256)} %get-tuple-element.330) | copy-start | bytes 3076
  412.4 10.4 %copy-start.27 = (f32[256]{0:T(256)S(1)}, f32[256]{0:T(256)}, u32[]{:S(2)}) copy-start(f32[256]{0:T(256)} %get-tuple-element.331) | copy-start | bytes 3076
  412.4 10.4 %copy-start.28 = (f32[256]{0:T(256)S(1)}, f32[256]{0:T(256)}, u32[]{:S(2)}) copy-start(f32[256]{0:T(256)} %get-tuple-element.332) | copy-start | bytes 3076
  412.4 10.4 %copy-start.29 = (f32[256]{0:T(256)S(1)}, f32[256]{0:T(256)}, u32[]{:S(2)}) copy-start(f32[256]{0:T(256)} %get-tuple-element.333) | copy-start | bytes 3076
  412.4 10.4 %copy-start.30 = (f32[256]{0:T(256)S(1)}, f32[256]{0:T(256)}, u32[]{:S(2)}) copy-start(f32[256]{0:T(256)} %get-tuple-element.334) | copy-start | bytes 3076
  412.4 10.4 %copy-start.31 = (f32[256]{0:T(256)S(1)}, f32[256]{0:T(256)}, u32[]{:S(2)}) copy-start(f32[256]{0:T(256)} %get-tuple-element.335) | copy-start | bytes 3076
  415.3 9.7 %copy-start.67 = (f32[256]{0:T(256)S(1)}, f32[256]{0:T(256)}, u32[]{:S(2)}) copy-start(f32[256]{0:T(256)} %get-tuple-element.337) | copy-start | bytes 3076
  415.3 9.6 %copy-start.68 = (f32[256]{0:T(256)S(1)}, f32[256]{0:T(256)}, u32[]{:S(2)}) copy-start(f32[256]{0:T(256)} %get-tuple-element.355) | copy-start | bytes 3076
  415.3 9.6 %copy-start.69 = (f32[256]{0:T(256)S(1)}, f32[256]{0:T(256)}, u32[]{:S(2)}) copy-start(f32[256]{0:T(256)} %get-tuple-element.356) | copy-start | bytes 3076
  415.3 9.6 %copy-start.70 = (f32[256]{0:T(256)S(1)}, f32[256]{0:T(256)}, u32[]{:S(2)}) copy-start(f32[256]{0:T(256)} %get-tuple-element.357) | copy-start | bytes 3076
  417.6 9.6 %copy-start.4 = (f32[256,768]{0,1:T(8,128)S(1)}, f32[256,768]{0,1:T(8,128)}, u32[]{:S(2)}) copy-start(f32[256,768]{0,1:T(8,128)} %copy.52) | copy-start | bytes 2359300
  428.7 55.0 %copy-start.40 = (f32[768]{0:T(1024)S(1)}, f32[768]{0:T(1024)}, u32[]{:S(2)}) copy-start(f32[768]{0:T(1024)} %get-tuple-element.184) | copy-start | bytes 9220
  428.8 55.0 %copy-start.39 = (f32[768]{0:T(1024)S(1)}, f32[768]{0:T(1024)}, u32[]{:S(2)}) copy-start(f32[768]{0:T(1024)} %get-tuple-element.183) | copy-start | bytes 9220
  428.8 55.0 %copy-start.38 = (f32[768]{0:T(1024)S(1)}, f32[768]{0:T(1024)}, u32[]{:S(2)}) copy-start(f32[768]{0:T(1024)} %get-tuple-element.182) | copy-start | bytes 9220
  428.8 62.2 %copy-start.9 = (bf16[256,768]{1,0:T(8,128)(2,1)S(1)}, bf16[256,768]{1,0:T(8,128)(2,1)}, u32[]{:S(2)}) copy-start(bf16[256,768]{1,0:T(8,128)(2,1)} %copy-done.8) | copy-start | bytes 1179652
  428.8 62.2 %copy-start.12 = (bf16[256,768]{1,0:T(8,128)(2,1)S(1)}, bf16[256,768]{1,0:T(8,128)(2,1)}, u32[]{:S(2)}) copy-start(bf16[256,768]{1,0:T(8,128)(2,1)} %copy-done.11) | copy-start | bytes 1179652
  431.1 61.7 %copy-start.7 = (bf16[256,768]{1,0:T(8,128)(2,1)S(1)}, bf16[256,768]{1,0:T(8,128)(2,1)}, u32[]{:S(2)}) copy-start(bf16[256,768]{1,0:T(8,128)(2,1)} %param.21) | copy-start | bytes 1179652
  494.8 36.5 %copy-start.32 = (f32[768]{0:T(1024)S(1)}, f32[768]{0:T(1024)}, u32[]{:S(2)}) copy-start(f32[768]{0:T(1024)} %get-tuple-element.193) | copy-start | bytes 9220
  494.8 36.5 %copy-start.33 = (f32[768]{0:T(1024)S(1)}, f32[768]{0:T(1024)}, u32[]{:S(2)}) copy-start(f32[768]{0:T(1024)} %get-tuple-element.196) | copy-start | bytes 9220
  494.8 36.5 %copy-start.34 = (f32[768]{0:T(1024)S(1)}, f32[768]{0:T(1024)}, u32[]{:S(2)}) copy-start(f32[768]{0:T(1024)} %get-tuple-element.284) | copy-start | bytes 9220
  494.9 36.5 %copy-start.35 = (f32[768]{0:T(1024)S(1)}, f32[768]{0:T(1024)}, u32[]{:S(2)}) copy-start(f32[768]{0:T(1024)} %get-tuple-element.126) | copy-start | bytes 9220
  494.9 36.5 %copy-start.36 = (f32[768]{0:T(1024)S(1)}, f32[768]{0:T(1024)}, u32[]{:S(2)}) copy-start(f32[768]{0:T(1024)} %get-tuple-element.195) | copy-start | bytes 9220
  494.9 36.5 %copy-start.37 = (f32[768]{0:T(1024)S(1)}, f32[768]{0:T(1024)}, u32[]{:S(2)}) copy-start(f32[768]{0:T(1024)} %get-tuple-element.286) | copy-start | bytes 9220
  494.9 101.4 %copy-start.3 = (f32[256,768]{1,0:T(8,128)S(1)}, f32[256,768]{1,0:T(8,128)}, u32[]{:S(2)}) copy-start(f32[256,768]{1,0:T(8,128)} %copy-done.2) | copy-start | bytes 2359300
  494.9 101.4 %copy-start.81 = (f32[256]{0:T(256)S(1)}, f32[256]{0:T(256)}, u32[]{:S(2)}) copy-start(f32[256]{0:T(256)} %copy-done.80) | copy-start | bytes 3076
  494.9 248.0 %all-gather.9.cloned.1.call-start = ((), (), s32[]{:S(2)}) async-start(), calls=%async_computation.7 | async-start | bytes 10027008 | tf_op jit(solution)/shard_map/all_gather | solution.py:13
  (49 other events, 234.7 us)
Sparse Core Ops, SparseCore 0:
  83.6 65.6 all-gather.4
  165.6 76.4 reduce-scatter.2
  249.4 62.3 all-gather.6
  323.9 76.4 reduce-scatter.4
  402.8 115.1 all-reduce.7
  524.9 160.1 all-reduce.9
  686.7 56.1 all-gather.8
